TPU v7x, 512 devices: a whole 4x4x16 slice. The times are simulated.
512 devices in a mesh: lon: 16 (over z), lat: 8 (over x, y_lo), ens: 4 (over y_hi, core).
Axes of the slice: x: 4, y: 4 (y_hi: 2, y_lo: 2; y = y_hi * 2 + y_lo), z: 16, core: 2. Of those that a mesh axis runs over, the one named last changes fastest.
Arguments:
- field: bfloat16 [4, 128, 1024, 128], P('ens', 'lat', 'lon'), may hold values from -6 to 6
- cotangent: bfloat16 [4, 128, 1024, 128], P('ens', 'lat', 'lon'), may hold values from -6 to 6
- land_mask: int32 [128, 1024], P('lat', 'lon'), may hold values from 0 to 1, as said below
- kernel_taps: float32 [49, 128], replicated, may hold values from -0.875 to 0.875
- norm_gain: float32 [128], replicated, may hold values from 0.1 to 1.9
- norm_shift: float32 [128], replicated, may hold values from -3 to 3
- up_weight: bfloat16 [128, 256], replicated, may hold values from -0.5 to 0.5
- down_weight: bfloat16 [256, 128], replicated, may hold values from -0.375 to 0.375
Outputs:
- output: bfloat16 [4, 128, 1024, 128], P('ens', 'lat', 'lon')
- field_grad: bfloat16 [4, 128, 1024, 128], P('ens', 'lat', 'lon')
- kernel_grad: float32 [49, 128], replicated
- norm_grad: float32 [2, 128], replicated
- up_grad: float32 [128, 256], replicated
- down_grad: float32 [256, 128], replicated
Inputs may be any that keep to these rules, and one draw needn't show every extreme that they name: `land_mask`: 1 marks an ocean cell and 0 a land cell; the share of ocean differs from tile to tile.
All inputs are finite; a program needn't handle non-finite values.
Results may differ from a plain program's by a relative error of at most 0.0062.
Values may be sent and summed in bfloat16 or wider, within the bound.
A program may use at most 64 MiB of HBM per device.

v0:
```python
import math
import jax
import jax.numpy as jnp
from jax import lax
from jax.sharding import PartitionSpec as P

KERNEL = 7
DILATION = 2
REACH = 6


def partner(shard, axis, bit):
    return lax.ppermute(shard, axis, [(i, i ^ 1 << bit) for i in range(lax.axis_size(axis))])


def extended_2(cells, sides, width, closed):
    for axis, dim in sides:
        count = lax.axis_size(axis)
        ends = count if closed else count - 1
        head = lax.slice_in_dim(cells, 0, width, axis=dim)
        tail = lax.slice_in_dim(cells, cells.shape[dim] - width, cells.shape[dim], axis=dim)
        cells = jnp.concatenate(
            [
                lax.ppermute(tail, axis, [(i, (i + 1) % count) for i in range(ends)]),
                cells,
                lax.ppermute(head, axis, [((i + 1) % count, i) for i in range(ends)]),
            ],
            axis=dim,
        )
    return cells


def shifted(block, axis, distance):
    devices = range(lax.axis_size(axis))
    route = [((i - distance) % len(devices), i) for i in devices]
    return lax.ppermute(block, axis, route)


def passed_along(value, axis, steps):
    count = lax.axis_size(axis)
    leading, last = (max(0, -steps), min(count, count - steps))
    return lax.ppermute(value, axis, [(source, source + steps) for source in range(leading, last)])


def depthwise(widened, kernel_taps, rows, cols):
    total = jnp.zeros((rows, cols, widened.shape[2]), jnp.float32)
    for row_tap in range(KERNEL):
        for col_tap in range(KERNEL):
            window = widened[
                DILATION * row_tap : DILATION * row_tap + rows,
                DILATION * col_tap : DILATION * col_tap + cols,
            ]
            total = total + kernel_taps[row_tap * KERNEL + col_tap] * window
    return total


def fold_forward(strip):
    for bit_pos in range(lax.axis_size("lon").bit_length() - 1):
        strip = partner(strip, "lon", bit_pos)
    return strip


def fold_backward(strip):
    for bit_pos in range(lax.axis_size("lon").bit_length() - 1):
        strip = partner(strip.astype(jnp.bfloat16), "lon", bit_pos).astype(strip.dtype)
    return strip


def is_northern():
    return lax.axis_index("lat") == lax.axis_size("lat") - 1


def extend_rows(block):
    padded = extended_2(block, (("lat", 0),), REACH, False)
    height = block.shape[0]
    folded = fold_forward(block[height - REACH :][::-1, ::-1])
    upper = jnp.where(is_northern(), folded, padded[height + REACH :])
    return jnp.concatenate([padded[: height + REACH], upper], 0)


def extend_cols(block):
    return extended_2(block, (("lon", 1),), REACH, True)


def retract_cols(grads):
    width = grads.shape[1] - 2 * REACH
    own = grads[:, REACH : REACH + width]
    from_east = shifted(grads[:, :REACH].astype(jnp.bfloat16), "lon", -1).astype(jnp.float32)
    from_west = shifted(grads[:, REACH + width :].astype(jnp.bfloat16), "lon", 1).astype(
        jnp.float32
    )
    own = own.at[:, width - REACH :].add(from_east)
    return own.at[:, :REACH].add(from_west)


def retract_rows(grads):
    height = grads.shape[0] - 2 * REACH
    own = grads[REACH : REACH + height]
    upper = grads[REACH + height :]
    from_north = passed_along(grads[:REACH].astype(jnp.bfloat16), "lat", -1).astype(jnp.float32)
    from_south = passed_along(upper.astype(jnp.bfloat16), "lat", 1).astype(upper.dtype)
    folded = fold_backward(upper[::-1, ::-1])
    own = own.at[height - REACH :].add(from_north + jnp.where(is_northern(), folded, 0.0))
    return own.at[:REACH].add(from_south)


def shards(field, cotangent, land_mask, kernel_taps, norm_gain, norm_shift, up_weight, down_weight):
    state = field[0]
    upstream_in = cotangent[0]
    rows, cols, channels = state.shape
    sea = land_mask.astype(jnp.float32)[:, :, None]
    masked = (state.astype(jnp.float32) * sea).astype(jnp.bfloat16)
    extended = extend_cols(extend_rows(masked))
    widened = extended.astype(jnp.float32)
    mixed = depthwise(widened, kernel_taps, rows, cols)
    centered = mixed - jnp.mean(mixed, -1, keepdims=True)
    rstd = lax.rsqrt(jnp.mean(centered * centered, -1, keepdims=True) + 1e-06)
    unit = centered * rstd
    normed = (unit * norm_gain + norm_shift).astype(jnp.bfloat16)
    cells = rows * cols
    flat_norm = normed.reshape(cells, channels)
    pre = jnp.dot(flat_norm, up_weight, preferred_element_type=jnp.float32)
    slope = math.sqrt(2.0 / math.pi)
    tanh_val = jnp.tanh(slope * (pre + 0.044715 * pre * pre * pre))
    activated = (0.5 * pre * (1.0 + tanh_val)).astype(jnp.bfloat16)
    product = jnp.dot(activated, down_weight, preferred_element_type=jnp.float32).reshape(
        rows, cols, channels
    )
    output = ((state.astype(jnp.float32) + product) * sea).astype(jnp.bfloat16)
    upstream = (upstream_in.astype(jnp.float32) * sea).astype(jnp.bfloat16)
    flat_up = upstream.reshape(cells, channels)
    down_part = jnp.dot(activated.T, flat_up, preferred_element_type=jnp.float32)
    act_grad = jnp.dot(flat_up, down_weight.T, preferred_element_type=jnp.float32)
    deriv = 0.5 * (1.0 + tanh_val) + 0.5 * pre * (1.0 - tanh_val * tanh_val) * slope * (
        1.0 + 3.0 * 0.044715 * pre * pre
    )
    pre_grad = (act_grad * deriv).astype(jnp.bfloat16)
    up_part = jnp.dot(flat_norm.T, pre_grad, preferred_element_type=jnp.float32)
    norm_in_grad = jnp.dot(pre_grad, up_weight.T, preferred_element_type=jnp.float32).reshape(
        rows, cols, channels
    )
    norm_part = jnp.stack([jnp.sum(norm_in_grad * unit, (0, 1)), jnp.sum(norm_in_grad, (0, 1))])
    count = cells * lax.axis_size("lon") * lax.axis_size("lat") * lax.axis_size("ens")
    factor = 1.0 / math.sqrt(count)
    scaled = norm_in_grad * norm_gain
    mixed_grad = rstd * (
        scaled
        - jnp.mean(scaled, -1, keepdims=True)
        - unit * jnp.mean(scaled * unit, -1, keepdims=True)
    )
    kernel_rows = []
    for row_tap in range(KERNEL):
        for col_tap in range(KERNEL):
            window = widened[
                DILATION * row_tap : DILATION * row_tap + rows,
                DILATION * col_tap : DILATION * col_tap + cols,
            ]
            kernel_rows.append(jnp.sum(window * mixed_grad, (0, 1)))
    kernel_part = jnp.stack(kernel_rows)
    margin = 2 * REACH
    spread_grad = jnp.pad(mixed_grad, ((margin, margin), (margin, margin), (0, 0)))
    extended_grad = jnp.zeros((rows + margin, cols + margin, channels), jnp.float32)
    for row_tap in range(KERNEL):
        for col_tap in range(KERNEL):
            row_start = margin - DILATION * row_tap
            col_start = margin - DILATION * col_tap
            window = spread_grad[
                row_start : row_start + rows + margin, col_start : col_start + cols + margin
            ]
            extended_grad = extended_grad + kernel_taps[row_tap * KERNEL + col_tap] * window
    masked_grad = retract_rows(retract_cols(extended_grad))
    field_grad = ((upstream_in.astype(jnp.float32) + masked_grad) * sea).astype(jnp.bfloat16)
    kernel_sum, norm_sum, up_sum, down_sum = lax.psum(
        (kernel_part, norm_part, up_part, down_part), ("lon", "lat", "ens")
    )
    return (
        output[None],
        field_grad[None],
        kernel_sum * factor,
        norm_sum * factor,
        up_sum * factor,
        down_sum * factor,
    )


def solution(mesh):
    in_specs = (
        P("ens", "lat", "lon", None),
        P("ens", "lat", "lon", None),
        P("lat", "lon"),
        P(),
        P(),
        P(),
        P(),
        P(),
    )
    out_specs = (P("ens", "lat", "lon", None), P("ens", "lat", "lon", None), P(), P(), P(), P())
    return jax.shard_map(shards, mesh=mesh, in_specs=in_specs, out_specs=out_specs, check_vma=False)
```

profile of v0, /device:TPU:36, one launch (start us, length us, event | category | flops | bytes accessed | tf_op | source)
XLA Modules:
  0.0 698.0 jit_solution(13167900297526407773)
XLA Ops:
  7.3 0.8 convert_element_type.87
  8.0 1.1 fusion.106
  9.2 2.0 collective-permute-start.1
  11.3 3.5 collective-permute-start
  14.7 3.3 collective-permute-start.5
  18.1 5.2 collective-permute-start.2
  23.3 0.2 fusion.107
  23.5 2.4 collective-permute-done.2
  25.9 9.1 %collective-permute-start.3 = (bf16[6,64,128]{2,1,0:T(8,128)(2,1)S(1)}, bf16[6,64,128]{2,1,0:T(8,128)(2,1)S(1)}, u32[]{:S(2)}, u32[]{:S(2)}) collective-permute-start(bf16[6,64,128]{2,1,0:T(8,128)(2,1)S(1)} %collective-permute-done.2), channel_id=1, source_target_pairs={{0,128},{32,160},{64,192},{96,224},{128,0},{160,32},{192,64},{224,... | collective-permute-start | bytes 294920 | tf_op jit(solution)/shard_map/ppermute | solution.py:13
  35.0 4.4 collective-permute-done.3
  39.4 14.6 %collective-permute-start.4 = (bf16[6,64,128]{2,1,0:T(8,128)(2,1)S(1)}, bf16[6,64,128]{2,1,0:T(8,128)(2,1)S(1)}, u32[]{:S(2)}, u32[]{:S(2)}) collective-permute-start(bf16[6,64,128]{2,1,0:T(8,128)(2,1)S(1)} %collective-permute-done.3), channel_id=1, source_target_pairs={{0,256},{32,288},{64,320},{96,352},{128,384},{160,416},{192,448},{... | collective-permute-start | bytes 294920 | tf_op jit(solution)/shard_map/ppermute | solution.py:13
  54.1 5.7 collective-permute-done.4
  59.8 1.9 collective-permute-start.6
  61.8 3.9 collective-permute-start.7
  65.9 1.9 collective-permute-done.7
  68.1 3.9 fusion.116
  72.0 0.4 multiply_reduce_fusion.52
  72.4 0.3 add_convert_fusion
  72.8 0.5 multiply_convert_fusion
  73.3 1.0 fusion.122
  74.3 0.3 fusion.120
  74.6 0.8 fusion
  75.4 0.9 fusion.121
  76.3 0.4 fusion.113
  76.8 0.5 multiply_reduce_fusion
  77.3 1.5 multiply_reduce_fusion.1
  78.8 0.7 multiply_reduce_fusion.37
  79.5 0.9 multiply_reduce_fusion.19
  80.4 10.4 %fusion.114 = (bf16[28,76,128]{2,1,0:T(8,128)(2,1)S(1)}, f32[28,76,128]{2,1,0:T(8,128)S(1)}) fusion(f32[128]{0:T(128)S(1)} %get-tuple-element.172, f32[128]{0:T(128)S(1)} %get-tuple-element.173, f32[128]{0:T(128)S(1)} %get-tuple-element.126, f32[128]{0:T(128)S(1)} %get-tuple-element.127, f32[128]{0:T(128)S(1)} %get-tuple-element.128, ...), kind=kLoop, calls=%fused_computation.297 | loop fusion | flops 26693632 | bytes 2183680 | tf_op jit(solution)/shard_map/convert.5
  90.8 0.9 fusion.104
  91.8 2.8 collective-permute-start.9
  94.5 5.5 collective-permute-start.8
  100.3 102.3 %all-reduce.1 = (f32[49,128]{1,0:T(8,128)S(1)}, f32[2,128]{1,0:T(2,128)S(1)}) all-reduce(f32[49,128]{1,0:T(8,128)S(1)} %stack.208, f32[2,128]{1,0:T(2,128)S(1)} %pad_maximum_fusion.3), channel_id=1, replica_groups=mesh['lon'=16,'lat'=8,'ens'=4] {'lon','lat','ens'}, use_global_device_ids=true, to_apply=%region_53.54 | all-reduce | flops 6528 | bytes 52224 | tf_op jit(solution)/shard_map/psum | solution.py:173
  202.9 0.2 scatter-add.15
  203.3 2.8 collective-permute-start.11
  206.0 0.6 broadcast_multiply_fusion.2
  206.7 3.1 collective-permute-done.11
  209.8 3.5 collective-permute-start.12
  213.3 0.6 broadcast_multiply_fusion.6
  213.9 2.8 collective-permute-start.15
  216.7 4.1 collective-permute-start.10
  220.8 6.5 collective-permute-start.13
  227.3 440.4 %all-reduce.5.cloned.1.call-done = (f32[128,256]{1,0:T(8,128)}, f32[256,128]{1,0:T(8,128)}) async-done(((f32[128,256]{1,0:T(8,128)}, f32[256,128]{1,0:T(8,128)}), (f32[128,256]{1,0:T(8,128)}, f32[256,128]{1,0:T(8,128)})) %all-reduce.5.cloned.1.call-update) | async-done | bytes 262160 | tf_op jit(solution)/shard_map/psum | solution.py:173
  667.7 1.6 broadcast_multiply_fusion.1
  669.3 9.2 %collective-permute-start.14 = (bf16[6,64,128]{2,1,0:T(8,128)(2,1)S(1)}, bf16[6,64,128]{2,1,0:T(8,128)(2,1)S(1)}, u32[]{:S(2)}, u32[]{:S(2)}) collective-permute-start(bf16[6,64,128]{2,1,0:T(8,128)(2,1)S(1)} %collective-permute-done.13), channel_id=1, source_target_pairs={{0,256},{32,288},{64,320},{96,352},{128,384},{160,416},{192,448},{... | collective-permute-start | bytes 294920 | tf_op jit(solution)/shard_map/ppermute | solution.py:13
  678.4 1.6 broadcast_multiply_fusion
  680.0 10.2 %collective-permute-done.14 = bf16[6,64,128]{2,1,0:T(8,128)(2,1)S(1)} collective-permute-done((bf16[6,64,128]{2,1,0:T(8,128)(2,1)S(1)}, bf16[6,64,128]{2,1,0:T(8,128)(2,1)S(1)}, u32[]{:S(2)}, u32[]{:S(2)}) %collective-permute-start.14) | collective-permute-done | bytes 98336 | tf_op jit(solution)/shard_map/ppermute | solution.py:13
  690.3 0.9 fusion.110
  (54 shorter events, 1.5 us)
Async XLA Ops:
  7.2 65.6 %copy-start = (bf16[128,256]{1,0:T(8,128)(2,1)S(1)}, bf16[128,256]{1,0:T(8,128)(2,1)}, u32[]{:S(2)}) copy-start(bf16[128,256]{1,0:T(8,128)(2,1)} %param.22) | copy-start | bytes 196612
  7.2 16.1 %copy-start.2 = (bf16[1,16,64,128]{3,2,1,0:T(8,128)(2,1)S(1)}, bf16[1,16,64,128]{3,2,1,0:T(8,128)(2,1)}, u32[]{:S(2)}) copy-start(bf16[1,16,64,128]{3,2,1,0:T(8,128)(2,1)} %param.17) | copy-start | bytes 786436
  7.2 27.8 %copy-start.5 = (f32[49,128]{1,0:T(8,128)S(1)}, f32[49,128]{1,0:T(8,128)}, u32[]{:S(2)}) copy-start(f32[49,128]{1,0:T(8,128)} %param.19) | copy-start | bytes 75268
  7.2 660.5 %all-reduce.5.cloned.1.call-start = ((), (), s32[]{:S(2)}) async-start(), calls=%async_computation | async-start | bytes 524288 | tf_op jit(solution)/shard_map/psum | solution.py:173
  9.2 8.9 %collective-permute-start.1 = (bf16[6,64,128]{2,1,0:T(8,128)(2,1)S(1)}, bf16[6,64,128]{2,1,0:T(8,128)(2,1)S(1)}, u32[]{:S(2)}, u32[]{:S(2)}) collective-permute-start(bf16[6,64,128]{2,1,0:T(8,128)(2,1)S(1)} %rev.6), channel_id=1, source_target_pairs={{0,32},{32,0},{64,96},{96,64},{128,160},{160,128},{192,224},{224,1... | collective-permute-start | bytes 294920 | tf_op jit(solution)/shard_map/ppermute | solution.py:13
  11.3 48.5 %collective-permute-start = (bf16[6,64,128]{2,1,0:T(8,128)(2,1)S(1)}, bf16[6,64,128]{2,1,0:T(8,128)(2,1)S(1)}, u32[]{:S(2)}, u32[]{:S(2)}) collective-permute-start(bf16[6,64,128]{2,1,0:T(8,128)(2,1)S(1)} %get-tuple-element.124), channel_id=1, source_target_pairs={{0,4},{4,8},{8,12},{12,16},{16,20},{20,24},{24,28},{1,5},{5,9},{9,... | collective-permute-start | bytes 294920 | tf_op jit(solution)/shard_map/ppermute | solution.py:24
  14.7 39.3 %collective-permute-start.5 = (bf16[6,64,128]{2,1,0:T(8,128)(2,1)S(1)}, bf16[6,64,128]{2,1,0:T(8,128)(2,1)S(1)}, u32[]{:S(2)}, u32[]{:S(2)}) collective-permute-start(bf16[6,64,128]{2,1,0:T(8,128)(2,1)S(1)} %get-tuple-element.123), channel_id=1, source_target_pairs={{4,0},{8,4},{12,8},{16,12},{20,16},{24,20},{28,24},{5,1},{9,5},{13... | collective-permute-start | bytes 294920 | tf_op jit(solution)/shard_map/ppermute | solution.py:26
  18.1 7.8 %collective-permute-start.2 = (bf16[6,64,128]{2,1,0:T(8,128)(2,1)S(1)}, bf16[6,64,128]{2,1,0:T(8,128)(2,1)S(1)}, u32[]{:S(2)}, u32[]{:S(2)}) collective-permute-start(bf16[6,64,128]{2,1,0:T(8,128)(2,1)S(1)} %collective-permute-done.1), channel_id=1, source_target_pairs={{0,64},{32,96},{64,0},{96,32},{128,192},{160,224},{192,128},{224,1... | collective-permute-start | bytes 294920 | tf_op jit(solution)/shard_map/ppermute | solution.py:13
  25.9 13.5 %collective-permute-start.3 = (bf16[6,64,128]{2,1,0:T(8,128)(2,1)S(1)}, bf16[6,64,128]{2,1,0:T(8,128)(2,1)S(1)}, u32[]{:S(2)}, u32[]{:S(2)}) collective-permute-start(bf16[6,64,128]{2,1,0:T(8,128)(2,1)S(1)} %collective-permute-done.2), channel_id=1, source_target_pairs={{0,128},{32,160},{64,192},{96,224},{128,0},{160,32},{192,64},{224,... | collective-permute-start | bytes 294920 | tf_op jit(solution)/shard_map/ppermute | solution.py:13
  39.4 20.4 %collective-permute-start.4 = (bf16[6,64,128]{2,1,0:T(8,128)(2,1)S(1)}, bf16[6,64,128]{2,1,0:T(8,128)(2,1)S(1)}, u32[]{:S(2)}, u32[]{:S(2)}) collective-permute-start(bf16[6,64,128]{2,1,0:T(8,128)(2,1)S(1)} %collective-permute-done.3), channel_id=1, source_target_pairs={{0,256},{32,288},{64,320},{96,352},{128,384},{160,416},{192,448},{... | collective-permute-start | bytes 294920 | tf_op jit(solution)/shard_map/ppermute | solution.py:13
  59.8 6.1 collective-permute-start.6
  61.8 6.1 collective-permute-start.7
  68.0 4.4 copy-start.6
  68.0 4.4 copy-start.7
  72.8 1.5 copy-start.4
  80.4 10.5 %copy-start.1 = (bf16[1,16,64,128]{3,2,1,0:T(8,128)(2,1)S(1)}, bf16[1,16,64,128]{3,2,1,0:T(8,128)(2,1)}, u32[]{:S(2)}) copy-start(bf16[1,16,64,128]{3,2,1,0:T(8,128)(2,1)} %param.16) | copy-start | bytes 786436
  91.8 111.2 %collective-permute-start.9 = (bf16[28,6,128]{2,1,0:T(8,128)(2,1)S(1)}, bf16[28,6,128]{2,1,0:T(8,128)(2,1)S(1)}, u32[]{:S(2)}, u32[]{:S(2)}) collective-permute-start(bf16[28,6,128]{2,1,0:T(8,128)(2,1)S(1)} %get-tuple-element.119), channel_id=1, source_target_pairs={{480,0},{0,32},{32,64},{64,96},{96,128},{128,160},{160,192},{192,2... | collective-permute-start | bytes 129032 | tf_op jit(solution)/shard_map/ppermute | solution.py:36
  94.5 108.1 %collective-permute-start.8 = (bf16[28,6,128]{2,1,0:T(8,128)(2,1)S(1)}, bf16[28,6,128]{2,1,0:T(8,128)(2,1)S(1)}, u32[]{:S(2)}, u32[]{:S(2)}) collective-permute-start(bf16[28,6,128]{2,1,0:T(8,128)(2,1)S(1)} %get-tuple-element.120), channel_id=1, source_target_pairs={{32,0},{64,32},{96,64},{128,96},{160,128},{192,160},{224,192},{256... | collective-permute-start | bytes 129032 | tf_op jit(solution)/shard_map/ppermute | solution.py:36
  203.3 6.5 collective-permute-start.11
  209.8 11.0 %collective-permute-start.12 = (bf16[6,64,128]{2,1,0:T(8,128)(2,1)S(1)}, bf16[6,64,128]{2,1,0:T(8,128)(2,1)S(1)}, u32[]{:S(2)}, u32[]{:S(2)}) collective-permute-start(bf16[6,64,128]{2,1,0:T(8,128)(2,1)S(1)} %collective-permute-done.11), channel_id=1, source_target_pairs={{0,64},{32,96},{64,0},{96,32},{128,192},{160,224},{192,128},{224,1... | collective-permute-start | bytes 294920 | tf_op jit(solution)/shard_map/ppermute | solution.py:13
  213.8 476.4 %copy-start.3 = (bf16[1,16,64,128]{3,2,1,0:T(8,128)(2,1)S(1)}, bf16[1,16,64,128]{3,2,1,0:T(8,128)(2,1)}, u32[]{:S(2)}) copy-start(bf16[1,16,64,128]{3,2,1,0:T(8,128)(2,1)} %param.17) | copy-start | bytes 786436
  213.9 476.3 %collective-permute-start.15 = (bf16[6,64,128]{2,1,0:T(8,128)(2,1)S(1)}, bf16[6,64,128]{2,1,0:T(8,128)(2,1)S(1)}, u32[]{:S(2)}, u32[]{:S(2)}) collective-permute-start(bf16[6,64,128]{2,1,0:T(8,128)(2,1)S(1)} %get-tuple-element.116), channel_id=1, source_target_pairs={{0,4},{4,8},{8,12},{12,16},{16,20},{20,24},{24,28},{1,5},{5,9},{9,... | collective-permute-start | bytes 294920 | tf_op jit(solution)/shard_map/ppermute | solution.py:42
  216.7 463.3 %collective-permute-start.10 = (bf16[6,64,128]{2,1,0:T(8,128)(2,1)S(1)}, bf16[6,64,128]{2,1,0:T(8,128)(2,1)S(1)}, u32[]{:S(2)}, u32[]{:S(2)}) collective-permute-start(bf16[6,64,128]{2,1,0:T(8,128)(2,1)S(1)} %get-tuple-element.118), channel_id=1, source_target_pairs={{4,0},{8,4},{12,8},{16,12},{20,16},{24,20},{28,24},{5,1},{9,5},{13... | collective-permute-start | bytes 294920 | tf_op jit(solution)/shard_map/ppermute | solution.py:42
  220.8 448.5 %collective-permute-start.13 = (bf16[6,64,128]{2,1,0:T(8,128)(2,1)S(1)}, bf16[6,64,128]{2,1,0:T(8,128)(2,1)S(1)}, u32[]{:S(2)}, u32[]{:S(2)}) collective-permute-start(bf16[6,64,128]{2,1,0:T(8,128)(2,1)S(1)} %collective-permute-done.12), channel_id=1, source_target_pairs={{0,128},{32,160},{64,192},{96,224},{128,0},{160,32},{192,64},{224,... | collective-permute-start | bytes 294920 | tf_op jit(solution)/shard_map/ppermute | solution.py:13
  669.3 20.9 %collective-permute-start.14 = (bf16[6,64,128]{2,1,0:T(8,128)(2,1)S(1)}, bf16[6,64,128]{2,1,0:T(8,128)(2,1)S(1)}, u32[]{:S(2)}, u32[]{:S(2)}) collective-permute-start(bf16[6,64,128]{2,1,0:T(8,128)(2,1)S(1)} %collective-permute-done.13), channel_id=1, source_target_pairs={{0,256},{32,288},{64,320},{96,352},{128,384},{160,416},{192,448},{... | collective-permute-start | bytes 294920 | tf_op jit(solution)/shard_map/ppermute | solution.py:13
Sparse Core Ops, SparseCore 0:
  206.8 460.8 all-reduce.4
where the time goes:
time: 699 us; the launch traced here: 698 us
  waiting for transfers between devices  468 us (67%)
  blocking collectives  102 us (15%)
  starting transfers between devices  80.6 us (12%)
  other arithmetic  27.3 us (4%)
  between operations  14.5 us (2%)
    psum x1, waiting for transfers between devices, shards(): lax.psum((kernel_part, norm_part, up_part, down_part), ('lon', 'lat', 'en...  440 us
    psum x1, blocking collectives, shards(): lax.psum((kernel_part, norm_part, up_part, down_part), ('lon', 'lat', 'en...  102 us
    ppermute x8, starting transfers between devices, partner(): lax.ppermute(shard, axis, [(i, i ^ 1 << bit) for i in range(lax.axis_size...  52.8 us
    ppermute x8, waiting for transfers between devices, partner(): lax.ppermute(shard, axis, [(i, i ^ 1 << bit) for i in range(lax.axis_size...  25.8 us
  transfers between devices with their start and end apart: 17, of which 8 were waited for; matrix products, arithmetic and copies ran while one was open for 1% of the time, Pallas kernels for 0%

commit v1 on v0

--- a/solution.py
+++ b/solution.py
@@ -7,6 +7,12 @@
 KERNEL = 7
 DILATION = 2
 REACH = 6
+
+
+def floor_draw(a0):
+    for jj in ("lon", ("lat", "ens")):
+        a0 = jax.lax.psum(a0, jj)
+    return a0
 
 
 def partner(shard, axis, bit):
@@ -170,8 +176,8 @@
             extended_grad = extended_grad + kernel_taps[row_tap * KERNEL + col_tap] * window
     masked_grad = retract_rows(retract_cols(extended_grad))
     field_grad = ((upstream_in.astype(jnp.float32) + masked_grad) * sea).astype(jnp.bfloat16)
-    kernel_sum, norm_sum, up_sum, down_sum = lax.psum(
-        (kernel_part, norm_part, up_part, down_part), ("lon", "lat", "ens")
+    kernel_sum, norm_sum, up_sum, down_sum = floor_draw(
+        (kernel_part, norm_part, up_part, down_part)
     )
     return (
         output[None],

time: 699 us -> 445 us (0.64)
  the two profiles are of different devices: /device:TPU:36 before, /device:TPU:1 now
where the time goes in v1:
time: 445 us; the launch traced here: 444 us
  blocking collectives  179 us (40%)
  waiting for transfers between devices  140 us (31%)
  starting transfers between devices  74.2 us (17%)
  other arithmetic  29.3 us (7%)
  between operations  15.2 us (3%)
    psum x2, blocking collectives, floor_draw(): a0 = jax.lax.psum(a0, jj)  179 us
    psum x2, waiting for transfers between devices, floor_draw(): a0 = jax.lax.psum(a0, jj)  119 us
    ppermute x8, starting transfers between devices, partner(): lax.ppermute(shard, axis, [(i, i ^ 1 << bit) for i in range(lax.axis_size...  50.8 us
    ppermute x8, waiting for transfers between devices, partner(): lax.ppermute(shard, axis, [(i, i ^ 1 << bit) for i in range(lax.axis_size...  18.2 us
    another operation x1, other arithmetic  10.3 us
  transfers between devices with their start and end apart: 18, of which 8 were waited for; matrix products, arithmetic and copies ran while one was open for 2% of the time, Pallas kernels for 0%

profile of v1, /device:TPU:1, one launch (start us, length us, event | category | flops | bytes accessed | tf_op | source)
XLA Modules:
  0.0 444.1 jit_solution(720135551529844497)
XLA Ops:
  7.2 0.8 convert_element_type.87
  8.0 1.1 fusion.106
  9.2 4.4 collective-permute-start.1
  13.6 3.2 collective-permute-start
  16.8 1.3 collective-permute-start.5
  18.2 4.9 %collective-permute-start.2 = (bf16[6,64,128]{2,1,0:T(8,128)(2,1)S(1)}, bf16[6,64,128]{2,1,0:T(8,128)(2,1)S(1)}, u32[]{:S(2)}, u32[]{:S(2)}) collective-permute-start(bf16[6,64,128]{2,1,0:T(8,128)(2,1)S(1)} %collective-permute-done.1), channel_id=1, source_target_pairs={{0,64},{32,96},{64,0},{96,32},{128,192},{160,224},{192,128},{224,1... | collective-permute-start | bytes 294920 | tf_op jit(solution)/shard_map/ppermute | solution.py:19
  23.3 2.6 collective-permute-done.2
  25.9 11.0 %collective-permute-start.3 = (bf16[6,64,128]{2,1,0:T(8,128)(2,1)S(1)}, bf16[6,64,128]{2,1,0:T(8,128)(2,1)S(1)}, u32[]{:S(2)}, u32[]{:S(2)}) collective-permute-start(bf16[6,64,128]{2,1,0:T(8,128)(2,1)S(1)} %collective-permute-done.2), channel_id=1, source_target_pairs={{0,128},{32,160},{64,192},{96,224},{128,0},{160,32},{192,64},{224,... | collective-permute-start | bytes 294920 | tf_op jit(solution)/shard_map/ppermute | solution.py:19
  36.9 7.3 %collective-permute-done.3 = bf16[6,64,128]{2,1,0:T(8,128)(2,1)S(1)} collective-permute-done((bf16[6,64,128]{2,1,0:T(8,128)(2,1)S(1)}, bf16[6,64,128]{2,1,0:T(8,128)(2,1)S(1)}, u32[]{:S(2)}, u32[]{:S(2)}) %collective-permute-start.3) | collective-permute-done | bytes 98336 | tf_op jit(solution)/shard_map/ppermute | solution.py:19
  44.2 11.7 %collective-permute-start.4 = (bf16[6,64,128]{2,1,0:T(8,128)(2,1)S(1)}, bf16[6,64,128]{2,1,0:T(8,128)(2,1)S(1)}, u32[]{:S(2)}, u32[]{:S(2)}) collective-permute-start(bf16[6,64,128]{2,1,0:T(8,128)(2,1)S(1)} %collective-permute-done.3), channel_id=1, source_target_pairs={{0,256},{32,288},{64,320},{96,352},{128,384},{160,416},{192,448},{... | collective-permute-start | bytes 294920 | tf_op jit(solution)/shard_map/ppermute | solution.py:19
  56.0 2.5 collective-permute-done.4
  58.5 1.9 collective-permute-start.6
  60.4 7.2 %collective-permute-start.7 = (bf16[28,6,128]{2,1,0:T(8,128)(2,1)S(1)}, bf16[28,6,128]{2,1,0:T(8,128)(2,1)S(1)}, u32[]{:S(2)}, u32[]{:S(2)}) collective-permute-start(bf16[28,6,128]{2,1,0:T(8,128)(2,1)S(1)} %get-tuple-element.126), channel_id=1, source_target_pairs={{32,0},{64,32},{96,64},{128,96},{160,128},{192,160},{224,192},{256... | collective-permute-start | bytes 129032 | tf_op jit(solution)/shard_map/ppermute | solution.py:32
  67.7 1.2 collective-permute-done.7
  69.1 3.9 fusion.116
  73.1 0.4 multiply_reduce_fusion.52
  73.5 0.3 add_convert_fusion
  73.9 0.5 multiply_convert_fusion
  74.6 1.0 fusion.122
  75.9 0.8 fusion
  76.6 0.4 fusion.113
  77.1 0.9 multiply_reduce_fusion
  78.0 2.1 multiply_reduce_fusion.1
  80.1 1.2 multiply_reduce_fusion.37
  81.3 1.5 multiply_reduce_fusion.19
  82.9 10.3 %fusion.114 = (bf16[28,76,128]{2,1,0:T(8,128)(2,1)S(1)}, f32[28,76,128]{2,1,0:T(8,128)S(1)}) fusion(f32[128]{0:T(128)S(1)} %get-tuple-element.176, f32[128]{0:T(128)S(1)} %get-tuple-element.177, f32[128]{0:T(128)S(1)} %get-tuple-element.130, f32[128]{0:T(128)S(1)} %get-tuple-element.131, f32[128]{0:T(128)S(1)} %get-tuple-element.132, ...), kind=kLoop, calls=%fused_computation.297 | loop fusion | flops 26693632 | bytes 2183680 | tf_op jit(solution)/shard_map/convert.5
  93.2 0.9 fusion.104
  94.2 5.1 %collective-permute-start.8 = (bf16[28,6,128]{2,1,0:T(8,128)(2,1)S(1)}, bf16[28,6,128]{2,1,0:T(8,128)(2,1)S(1)}, u32[]{:S(2)}, u32[]{:S(2)}) collective-permute-start(bf16[28,6,128]{2,1,0:T(8,128)(2,1)S(1)} %get-tuple-element.124), channel_id=1, source_target_pairs={{32,0},{64,32},{96,64},{128,96},{160,128},{192,160},{224,192},{256... | collective-permute-start | bytes 129032 | tf_op jit(solution)/shard_map/ppermute | solution.py:42
  99.2 0.9 fusion.121
  100.5 1.9 collective-permute-start.9
  103.1 1.5 stack.208
  104.8 1.9 collective-permute-done.9
  107.0 1.9 collective-permute-start.11
  109.0 42.1 %all-reduce.3 = (f32[49,128]{1,0:T(8,128)S(1)}, f32[2,128]{1,0:T(2,128)S(1)}) all-reduce(f32[49,128]{1,0:T(8,128)S(1)} %stack.208, f32[2,128]{1,0:T(2,128)S(1)} %pad_maximum_fusion.3), channel_id=1, replica_groups=mesh['lon'=16,'lat'=8,'ens'=4] {'lon'}, use_global_device_ids=true, to_apply=%region_53.54 | all-reduce | flops 6528 | bytes 52224 | tf_op jit(solution)/shard_map/psum | solution.py:14
  151.1 136.7 %all-reduce.1 = (f32[49,128]{1,0:T(8,128)S(1)}, f32[2,128]{1,0:T(2,128)S(1)}) all-reduce(f32[49,128]{1,0:T(8,128)S(1)} %get-tuple-element.111, f32[2,128]{1,0:T(2,128)S(1)} %get-tuple-element.112), channel_id=1, replica_groups=mesh['lon'=16,'lat'=8,'ens'=4] {'lat','ens'}, use_global_device_ids=true, to_apply=%region_54.55 | all-reduce | flops 6528 | bytes 52224 | tf_op jit(solution)/shard_map/psum | solution.py:14
  287.8 2.0 collective-permute-start.12
  289.8 0.6 broadcast_multiply_fusion.2
  290.4 3.6 collective-permute-done.12
  294.1 5.5 %collective-permute-start.13 = (bf16[6,64,128]{2,1,0:T(8,128)(2,1)S(1)}, bf16[6,64,128]{2,1,0:T(8,128)(2,1)S(1)}, u32[]{:S(2)}, u32[]{:S(2)}) collective-permute-start(bf16[6,64,128]{2,1,0:T(8,128)(2,1)S(1)} %collective-permute-done.12), channel_id=1, source_target_pairs={{0,128},{32,160},{64,192},{96,224},{128,0},{160,32},{192,64},{224,... | collective-permute-start | bytes 294920 | tf_op jit(solution)/shard_map/ppermute | solution.py:19
  299.7 0.6 broadcast_multiply_fusion.6
  300.3 1.4 collective-permute-start.15
  301.7 1.3 collective-permute-start.10
  303.0 2.2 collective-permute-done.13
  305.2 9.3 %collective-permute-start.14 = (bf16[6,64,128]{2,1,0:T(8,128)(2,1)S(1)}, bf16[6,64,128]{2,1,0:T(8,128)(2,1)S(1)}, u32[]{:S(2)}, u32[]{:S(2)}) collective-permute-start(bf16[6,64,128]{2,1,0:T(8,128)(2,1)S(1)} %collective-permute-done.13), channel_id=1, source_target_pairs={{0,256},{32,288},{64,320},{96,352},{128,384},{160,416},{192,448},{... | collective-permute-start | bytes 294920 | tf_op jit(solution)/shard_map/ppermute | solution.py:19
  314.5 118.5 %all-reduce.8.cloned.1.call-done = (f32[128,256]{1,0:T(8,128)}, f32[256,128]{1,0:T(8,128)}) async-done(((f32[128,256]{1,0:T(8,128)}, f32[256,128]{1,0:T(8,128)}), (f32[128,256]{1,0:T(8,128)}, f32[256,128]{1,0:T(8,128)})) %all-reduce.8.cloned.1.call-update) | async-done | bytes 262160 | tf_op jit(solution)/shard_map/psum | solution.py:14
  433.1 1.6 broadcast_multiply_fusion.1
  434.7 1.6 broadcast_multiply_fusion
  436.4 0.9 fusion.110
  (144 shorter events, 2.3 us)
Async XLA Ops:
  7.2 66.7 %copy-start = (bf16[128,256]{1,0:T(8,128)(2,1)S(1)}, bf16[128,256]{1,0:T(8,128)(2,1)}, u32[]{:S(2)}) copy-start(bf16[128,256]{1,0:T(8,128)(2,1)} %param.22) | copy-start | bytes 196612
  7.2 15.9 %copy-start.4 = (bf16[1,16,64,128]{3,2,1,0:T(8,128)(2,1)S(1)}, bf16[1,16,64,128]{3,2,1,0:T(8,128)(2,1)}, u32[]{:S(2)}) copy-start(bf16[1,16,64,128]{3,2,1,0:T(8,128)(2,1)} %param.17) | copy-start | bytes 786436
  7.2 29.7 %copy-start.7 = (f32[49,128]{1,0:T(8,128)S(1)}, f32[49,128]{1,0:T(8,128)}, u32[]{:S(2)}) copy-start(f32[49,128]{1,0:T(8,128)} %param.19) | copy-start | bytes 75268
  7.2 292.4 %all-reduce.10.cloned.1.call-start = ((), (), s32[]{:S(2)}) async-start(), calls=%async_computation.1 | async-start | bytes 524288 | tf_op jit(solution)/shard_map/psum | solution.py:14
  9.2 9.0 %collective-permute-start.1 = (bf16[6,64,128]{2,1,0:T(8,128)(2,1)S(1)}, bf16[6,64,128]{2,1,0:T(8,128)(2,1)S(1)}, u32[]{:S(2)}, u32[]{:S(2)}) collective-permute-start(bf16[6,64,128]{2,1,0:T(8,128)(2,1)S(1)} %rev.6), channel_id=1, source_target_pairs={{0,32},{32,0},{64,96},{96,64},{128,160},{160,128},{192,224},{224,1... | collective-permute-start | bytes 294920 | tf_op jit(solution)/shard_map/ppermute | solution.py:19
  13.6 44.9 %collective-permute-start = (bf16[6,64,128]{2,1,0:T(8,128)(2,1)S(1)}, bf16[6,64,128]{2,1,0:T(8,128)(2,1)S(1)}, u32[]{:S(2)}, u32[]{:S(2)}) collective-permute-start(bf16[6,64,128]{2,1,0:T(8,128)(2,1)S(1)} %get-tuple-element.128), channel_id=1, source_target_pairs={{0,4},{4,8},{8,12},{12,16},{16,20},{20,24},{24,28},{1,5},{5,9},{9,... | collective-permute-start | bytes 294920 | tf_op jit(solution)/shard_map/ppermute | solution.py:30
  16.8 39.1 %collective-permute-start.5 = (bf16[6,64,128]{2,1,0:T(8,128)(2,1)S(1)}, bf16[6,64,128]{2,1,0:T(8,128)(2,1)S(1)}, u32[]{:S(2)}, u32[]{:S(2)}) collective-permute-start(bf16[6,64,128]{2,1,0:T(8,128)(2,1)S(1)} %get-tuple-element.127), channel_id=1, source_target_pairs={{4,0},{8,4},{12,8},{16,12},{20,16},{24,20},{28,24},{5,1},{9,5},{13... | collective-permute-start | bytes 294920 | tf_op jit(solution)/shard_map/ppermute | solution.py:32
  18.2 7.7 %collective-permute-start.2 = (bf16[6,64,128]{2,1,0:T(8,128)(2,1)S(1)}, bf16[6,64,128]{2,1,0:T(8,128)(2,1)S(1)}, u32[]{:S(2)}, u32[]{:S(2)}) collective-permute-start(bf16[6,64,128]{2,1,0:T(8,128)(2,1)S(1)} %collective-permute-done.1), channel_id=1, source_target_pairs={{0,64},{32,96},{64,0},{96,32},{128,192},{160,224},{192,128},{224,1... | collective-permute-start | bytes 294920 | tf_op jit(solution)/shard_map/ppermute | solution.py:19
  25.9 18.3 %collective-permute-start.3 = (bf16[6,64,128]{2,1,0:T(8,128)(2,1)S(1)}, bf16[6,64,128]{2,1,0:T(8,128)(2,1)S(1)}, u32[]{:S(2)}, u32[]{:S(2)}) collective-permute-start(bf16[6,64,128]{2,1,0:T(8,128)(2,1)S(1)} %collective-permute-done.2), channel_id=1, source_target_pairs={{0,128},{32,160},{64,192},{96,224},{128,0},{160,32},{192,64},{224,... | collective-permute-start | bytes 294920 | tf_op jit(solution)/shard_map/ppermute | solution.py:19
  44.2 14.3 %collective-permute-start.4 = (bf16[6,64,128]{2,1,0:T(8,128)(2,1)S(1)}, bf16[6,64,128]{2,1,0:T(8,128)(2,1)S(1)}, u32[]{:S(2)}, u32[]{:S(2)}) collective-permute-start(bf16[6,64,128]{2,1,0:T(8,128)(2,1)S(1)} %collective-permute-done.3), channel_id=1, source_target_pairs={{0,256},{32,288},{64,320},{96,352},{128,384},{160,416},{192,448},{... | collective-permute-start | bytes 294920 | tf_op jit(solution)/shard_map/ppermute | solution.py:19
  58.5 9.2 %collective-permute-start.6 = (bf16[28,6,128]{2,1,0:T(8,128)(2,1)S(1)}, bf16[28,6,128]{2,1,0:T(8,128)(2,1)S(1)}, u32[]{:S(2)}, u32[]{:S(2)}) collective-permute-start(bf16[28,6,128]{2,1,0:T(8,128)(2,1)S(1)} %get-tuple-element.125), channel_id=1, source_target_pairs={{0,32},{32,64},{64,96},{96,128},{128,160},{160,192},{192,224},{224... | collective-permute-start | bytes 129032 | tf_op jit(solution)/shard_map/ppermute | solution.py:30
  60.4 8.5 %collective-permute-start.7 = (bf16[28,6,128]{2,1,0:T(8,128)(2,1)S(1)}, bf16[28,6,128]{2,1,0:T(8,128)(2,1)S(1)}, u32[]{:S(2)}, u32[]{:S(2)}) collective-permute-start(bf16[28,6,128]{2,1,0:T(8,128)(2,1)S(1)} %get-tuple-element.126), channel_id=1, source_target_pairs={{32,0},{64,32},{96,64},{128,96},{160,128},{192,160},{224,192},{256... | collective-permute-start | bytes 129032 | tf_op jit(solution)/shard_map/ppermute | solution.py:32
  69.1 4.4 copy-start.8
  69.1 4.4 copy-start.50
  82.8 10.4 %copy-start.3 = (bf16[1,16,64,128]{3,2,1,0:T(8,128)(2,1)S(1)}, bf16[1,16,64,128]{3,2,1,0:T(8,128)(2,1)}, u32[]{:S(2)}) copy-start(bf16[1,16,64,128]{3,2,1,0:T(8,128)(2,1)} %param.16) | copy-start | bytes 786436
  93.2 6.0 %copy-start.2 = (bf16[16,64,128]{2,1,0:T(8,128)(2,1)S(1)}, bf16[16,64,128]{2,1,0:T(8,128)(2,1)}, u32[]{:S(2)}) copy-start(bf16[16,64,128]{2,1,0:T(8,128)(2,1)} %copy-done.1) | copy-start | bytes 786436
  94.2 10.4 %collective-permute-start.8 = (bf16[28,6,128]{2,1,0:T(8,128)(2,1)S(1)}, bf16[28,6,128]{2,1,0:T(8,128)(2,1)S(1)}, u32[]{:S(2)}, u32[]{:S(2)}) collective-permute-start(bf16[28,6,128]{2,1,0:T(8,128)(2,1)S(1)} %get-tuple-element.124), channel_id=1, source_target_pairs={{32,0},{64,32},{96,64},{128,96},{160,128},{192,160},{224,192},{256... | collective-permute-start | bytes 129032 | tf_op jit(solution)/shard_map/ppermute | solution.py:42
  100.2 2.5 copy-start.13
  100.2 2.5 copy-start.14
  100.2 2.5 copy-start.15
  100.2 2.5 copy-start.16
  100.2 2.5 copy-start.17
  100.2 2.5 copy-start.18
  100.2 2.5 copy-start.19
  100.3 2.5 copy-start.20
  100.3 2.5 copy-start.21
  100.3 2.5 copy-start.22
  100.3 2.5 copy-start.23
  100.3 2.5 copy-start.24
  100.3 2.5 copy-start.25
  100.3 2.5 copy-start.26
  100.3 2.5 copy-start.27
  100.3 2.5 copy-start.28
  100.3 2.5 copy-start.29
  100.4 2.5 copy-start.30
  100.4 2.5 copy-start.31
  100.4 2.5 copy-start.32
  100.4 2.5 copy-start.33
  100.5 6.1 %collective-permute-start.9 = (bf16[28,6,128]{2,1,0:T(8,128)(2,1)S(1)}, bf16[28,6,128]{2,1,0:T(8,128)(2,1)S(1)}, u32[]{:S(2)}, u32[]{:S(2)}) collective-permute-start(bf16[28,6,128]{2,1,0:T(8,128)(2,1)S(1)} %get-tuple-element.123), channel_id=1, source_target_pairs={{480,0},{0,32},{32,64},{64,96},{96,128},{128,160},{160,192},{192,2... | collective-permute-start | bytes 129032 | tf_op jit(solution)/shard_map/ppermute | solution.py:42
  102.6 330.5 %all-reduce.8.cloned.1.call-start = ((), (), s32[]{:S(2)}) async-start(), calls=%async_computation | async-start | bytes 524288 | tf_op jit(solution)/shard_map/psum | solution.py:14
  104.5 4.4 copy-start.49
  107.0 180.8 %collective-permute-start.11 = (bf16[6,64,128]{2,1,0:T(8,128)(2,1)S(1)}, bf16[6,64,128]{2,1,0:T(8,128)(2,1)S(1)}, u32[]{:S(2)}, u32[]{:S(2)}) collective-permute-start(bf16[6,64,128]{2,1,0:T(8,128)(2,1)S(1)} %rev.7), channel_id=1, source_target_pairs={{0,32},{32,0},{64,96},{96,64},{128,160},{160,128},{192,224},{224,1... | collective-permute-start | bytes 294920 | tf_op jit(solution)/shard_map/ppermute | solution.py:19
  287.8 6.2 %collective-permute-start.12 = (bf16[6,64,128]{2,1,0:T(8,128)(2,1)S(1)}, bf16[6,64,128]{2,1,0:T(8,128)(2,1)S(1)}, u32[]{:S(2)}, u32[]{:S(2)}) collective-permute-start(bf16[6,64,128]{2,1,0:T(8,128)(2,1)S(1)} %collective-permute-done.11), channel_id=1, source_target_pairs={{0,64},{32,96},{64,0},{96,32},{128,192},{160,224},{192,128},{224,1... | collective-permute-start | bytes 294920 | tf_op jit(solution)/shard_map/ppermute | solution.py:19
  294.1 11.1 %collective-permute-start.13 = (bf16[6,64,128]{2,1,0:T(8,128)(2,1)S(1)}, bf16[6,64,128]{2,1,0:T(8,128)(2,1)S(1)}, u32[]{:S(2)}, u32[]{:S(2)}) collective-permute-start(bf16[6,64,128]{2,1,0:T(8,128)(2,1)S(1)} %collective-permute-done.12), channel_id=1, source_target_pairs={{0,128},{32,160},{64,192},{96,224},{128,0},{160,32},{192,64},{224,... | collective-permute-start | bytes 294920 | tf_op jit(solution)/shard_map/ppermute | solution.py:19
  300.2 136.1 %copy-start.5 = (bf16[1,16,64,128]{3,2,1,0:T(8,128)(2,1)S(1)}, bf16[1,16,64,128]{3,2,1,0:T(8,128)(2,1)}, u32[]{:S(2)}) copy-start(bf16[1,16,64,128]{3,2,1,0:T(8,128)(2,1)} %param.17) | copy-start | bytes 786436
  300.3 136.0 %collective-permute-start.15 = (bf16[6,64,128]{2,1,0:T(8,128)(2,1)S(1)}, bf16[6,64,128]{2,1,0:T(8,128)(2,1)S(1)}, u32[]{:S(2)}, u32[]{:S(2)}) collective-permute-start(bf16[6,64,128]{2,1,0:T(8,128)(2,1)S(1)} %get-tuple-element.120), channel_id=1, source_target_pairs={{0,4},{4,8},{8,12},{12,16},{16,20},{20,24},{24,28},{1,5},{5,9},{9,... | collective-permute-start | bytes 294920 | tf_op jit(solution)/shard_map/ppermute | solution.py:48
  301.7 134.5 %collective-permute-start.10 = (bf16[6,64,128]{2,1,0:T(8,128)(2,1)S(1)}, bf16[6,64,128]{2,1,0:T(8,128)(2,1)S(1)}, u32[]{:S(2)}, u32[]{:S(2)}) collective-permute-start(bf16[6,64,128]{2,1,0:T(8,128)(2,1)S(1)} %get-tuple-element.122), channel_id=1, source_target_pairs={{4,0},{8,4},{12,8},{16,12},{20,16},{24,20},{28,24},{5,1},{9,5},{13... | collective-permute-start | bytes 294920 | tf_op jit(solution)/shard_map/ppermute | solution.py:48
  305.2 131.0 %collective-permute-start.14 = (bf16[6,64,128]{2,1,0:T(8,128)(2,1)S(1)}, bf16[6,64,128]{2,1,0:T(8,128)(2,1)S(1)}, u32[]{:S(2)}, u32[]{:S(2)}) collective-permute-start(bf16[6,64,128]{2,1,0:T(8,128)(2,1)S(1)} %collective-permute-done.13), channel_id=1, source_target_pairs={{0,256},{32,288},{64,320},{96,352},{128,384},{160,416},{192,448},{... | collective-permute-start | bytes 294920 | tf_op jit(solution)/shard_map/ppermute | solution.py:19
  (21 other events, 50.2 us)
Sparse Core Ops, SparseCore 0:
  102.7 131.1 all-reduce.9
  299.8 133.2 all-reduce.7
